TPU v7x, 32 devices: a whole 2x2x4 slice. The times are simulated.
32 devices in a mesh: tm: 8 (over y, x, core), space: 4 (over z).
Axes of the slice: x: 2, y: 2, z: 4, core: 2. Of those that a mesh axis runs over, the one named last changes fastest.
Arguments:
- steps: bfloat16 [24, 1024, 1024], P('tm', 'space'), as said below
- lengths: int32 [8], P('tm'), may hold values from 1 to 3, 16 in all
- anchor: bfloat16 [1024, 2048], P(None, 'space'), may hold values from -6 to 6
Outputs:
- panels: float32 [24, 1024, 2048], P('tm', None, 'space')
Inputs may be any that keep to these rules, and one draw needn't show every extreme that they name: `steps`: slots of a section beyond its length hold entries that no output reads.
All inputs are finite; a program needn't handle non-finite values. No bound on the sum of `lengths` on one device may be relied on, other than what follows from the above.
Results may differ from a plain program's by a relative error of at most 0.025.
Values may be sent and summed in bfloat16 or wider, within the bound.
A program may use at most 64 MiB of HBM per device.

v0:
```python
import jax
import jax.numpy as jnp
from jax import lax
from jax.sharding import PartitionSpec as P


def from_behind(block, axis, distance):
    devices = range(lax.axis_size(axis))
    route = [(i - distance, i) for i in devices if i - distance in devices]
    return lax.ppermute(block, axis, route)


def run_section(blocks, section_count, incoming, results, offset):
    capacity = blocks.shape[0]
    for slot in range(capacity - 1, -1, -1):

        def live(state, slot=slot):
            carry_in, stored = state
            value = jnp.dot(blocks[slot], carry_in, preferred_element_type=jnp.float32)
            stored = lax.dynamic_update_slice(stored, value[None], (slot, 0, offset))
            return (value.astype(jnp.bfloat16), stored)

        incoming, results = lax.cond(
            slot < section_count, live, lambda state: state, (incoming, results)
        )
    return (incoming, results)


def shards(steps, lengths, anchor):
    capacity, width = (steps.shape[0], anchor.shape[1])
    rows = anchor.shape[0]
    segments = lax.axis_size("tm")
    me = lax.axis_index("tm")
    section_count = lengths[0]
    blocks = lax.all_gather(steps, "space", axis=1, tiled=True)
    results = jnp.zeros((capacity, rows, width), jnp.float32)

    def segment(k, state):
        incoming, stored = state
        active = me == segments - 1 - k
        incoming, stored = lax.cond(
            active,
            lambda s: run_section(blocks, section_count, s[0], s[1], 0),
            lambda s: s,
            (incoming, stored),
        )
        incoming = from_behind(incoming, "tm", -1)
        return (incoming, stored)

    final, results = lax.fori_loop(0, segments, segment, (anchor, results))
    return results


def solution(mesh):
    return jax.shard_map(
        shards,
        mesh=mesh,
        in_specs=(P("tm", "space", None), P("tm"), P(None, "space")),
        out_specs=P("tm", None, "space"),
        check_vma=False,
    )
```

profile of v0, /device:TPU:3, one launch (start us, length us, event | category | flops | bytes accessed | tf_op | source)
XLA Modules:
  0.0 303.0 jit_solution(14158469819239776622)
XLA Ops:
  6.5 0.7 all-gather.2.cloned.1.call-update
  7.3 118.4 %all-gather.2.cloned.1.call-done = bf16[3,1024,1024]{2,1,0:T(8,128)(2,1)} async-done(((bf16[3,256,1024]{2,1,0:T(8,128)(2,1)}), bf16[3,1024,1024]{2,1,0:T(8,128)(2,1)}) %all-gather.2.cloned.1.call-update) | async-done | bytes 6291472 | tf_op jit(solution)/shard_map/all_gather | solution.py:35
  125.7 3.5 %broadcast_in_dim.12 = f32[3,1024,512]{2,1,0:T(8,128)} broadcast(f32[]{:T(128)} %constant.39.clone.1), dimensions={} | broadcast | bytes 6291460 | tf_op jit(solution)/shard_map/broadcast_in_dim | solution.py:36
  129.2 167.0 %while.15 = (s32[]{:T(128)}, bf16[1024,512]{1,0:T(8,128)(2,1)S(1)}, f32[3,1024,512]{2,1,0:T(8,128)}, s32[]{:T(128)}, s32[]{:T(128)}, /*index=5*/bf16[3,1024,1024]{2,1,0:T(8,128)(2,1)}, s32[]{:T(128)}, s32[]{:T(128)}) while((s32[]{:T(128)}, bf16[1024,512]{1,0:T(8,128)(2,1)S(1)}, f32[3,1024,512]{2,1,0:T(8,128)}, s32[]{:T(128)}, s32[]{:T(128)}, ...), condition=%wide.region_9.0_spmd, body=%wide.region_0.0_spmd.sunk | while | flops 3222798336 | bytes 44040592 | solution.py:50
  129.2 2.4 collective-permute-start
  131.6 14.6 %collective-permute-done = bf16[1024,512]{1,0:T(8,128)(2,1)S(1)} collective-permute-done((bf16[1024,512]{1,0:T(8,128)(2,1)S(1)}, bf16[1024,512]{1,0:T(8,128)(2,1)S(1)}, u32[]{:S(2)}, u32[]{:S(2)}) %collective-permute-start) | collective-permute-done | bytes 1048608 | tf_op jit(solution)/shard_map/while/body/eval_jaxpr/ppermute | solution.py:10
  146.3 1.9 collective-permute-start
  148.2 15.1 %collective-permute-done = bf16[1024,512]{1,0:T(8,128)(2,1)S(1)} collective-permute-done((bf16[1024,512]{1,0:T(8,128)(2,1)S(1)}, bf16[1024,512]{1,0:T(8,128)(2,1)S(1)}, u32[]{:S(2)}, u32[]{:S(2)}) %collective-permute-start) | collective-permute-done | bytes 1048608 | tf_op jit(solution)/shard_map/while/body/eval_jaxpr/ppermute | solution.py:10
  163.4 1.9 collective-permute-start
  165.4 15.1 %collective-permute-done = bf16[1024,512]{1,0:T(8,128)(2,1)S(1)} collective-permute-done((bf16[1024,512]{1,0:T(8,128)(2,1)S(1)}, bf16[1024,512]{1,0:T(8,128)(2,1)S(1)}, u32[]{:S(2)}, u32[]{:S(2)}) %collective-permute-start) | collective-permute-done | bytes 1048608 | tf_op jit(solution)/shard_map/while/body/eval_jaxpr/ppermute | solution.py:10
  180.6 1.9 collective-permute-start
  182.5 29.8 %collective-permute-done = bf16[1024,512]{1,0:T(8,128)(2,1)S(1)} collective-permute-done((bf16[1024,512]{1,0:T(8,128)(2,1)S(1)}, bf16[1024,512]{1,0:T(8,128)(2,1)S(1)}, u32[]{:S(2)}, u32[]{:S(2)}) %collective-permute-start) | collective-permute-done | bytes 1048608 | tf_op jit(solution)/shard_map/while/body/eval_jaxpr/ppermute | solution.py:10
  212.4 15.3 %conditional.5 = ((bf16[1024,512]{1,0:T(8,128)(2,1)S(1)}, f32[3,1024,512]{2,1,0:T(8,128)})) conditional(s32[]{:T(128)} %convert_element_type.29, (bf16[1024,512]{1,0:T(8,128)(2,1)S(1)}, f32[3,1024,512]{2,1,0:T(8,128)}) %tuple.58, (s32[]{:T(128)}, bf16[1024,512]{1,0:T(8,128)(2,1)S(1)}, f32[3,1024,512]{2,1,0:T(8,128)}, ...), branch_computations={%region_1.0_spmd, %region_2.0_spmd} | conditional | flops 3222798336 | bytes 37748936 | solution.py:41
  213.1 4.4 %conditional = ((bf16[1024,512]{1,0:T(8,128)(2,1)S(1)}, f32[3,1024,512]{2,1,0:T(8,128)})) conditional(s32[]{:T(128)} %convert_element_type.23, (bf16[1024,512]{1,0:T(8,128)(2,1)S(1)}, f32[3,1024,512]{2,1,0:T(8,128)}) %tuple.36, (bf16[3,1024,1024]{2,1,0:T(8,128)(2,1)}, bf16[1024,512]{1,0:T(8,128)(2,1)S(1)}, f32[3,1024,512]{2,1,0:T(8,128)}) %tuple.37), branch_computations={%region_3.0_spmd, %region_4.0_spmd} | conditional | flops 1074266112 | bytes 12582936 | solution.py:23
  213.1 0.1 copy.32
  213.2 2.8 fusion.9
  216.0 1.5 bitcast_dynamic-update-slice_fusion
  218.2 4.4 %conditional.1 = ((bf16[1024,512]{1,0:T(8,128)(2,1)S(1)}, f32[3,1024,512]{2,1,0:T(8,128)})) conditional(s32[]{:T(128)} %convert_element_type.22, (bf16[1024,512]{1,0:T(8,128)(2,1)S(1)}, f32[3,1024,512]{2,1,0:T(8,128)}) %get-tuple-element.277, (bf16[3,1024,1024]{2,1,0:T(8,128)(2,1)}, bf16[1024,512]{1,0:T(8,128)(2,1)S(1)}, ...), branch_computations={%region_5.0_spmd, %region_6.0_spmd} | conditional | flops 1074266112 | bytes 12582936 | solution.py:23
  218.2 0.1 copy.33
  218.3 2.8 fusion.10
  221.1 1.5 bitcast_dynamic-update-slice_fusion.1
  223.3 4.4 %conditional.2 = ((bf16[1024,512]{1,0:T(8,128)(2,1)S(1)}, f32[3,1024,512]{2,1,0:T(8,128)})) conditional(s32[]{:T(128)} %convert_element_type.21, (bf16[1024,512]{1,0:T(8,128)(2,1)S(1)}, f32[3,1024,512]{2,1,0:T(8,128)}) %get-tuple-element.278, (bf16[3,1024,1024]{2,1,0:T(8,128)(2,1)}, bf16[1024,512]{1,0:T(8,128)(2,1)S(1)}, ...), branch_computations={%region_7.0_spmd, %region_8.0_spmd} | conditional | flops 1074266112 | bytes 12582936 | solution.py:23
  223.3 2.8 fusion.11
  226.2 1.5 bitcast_dynamic-update-slice_fusion.2
  227.7 1.9 collective-permute-start
  229.6 15.1 %collective-permute-done = bf16[1024,512]{1,0:T(8,128)(2,1)S(1)} collective-permute-done((bf16[1024,512]{1,0:T(8,128)(2,1)S(1)}, bf16[1024,512]{1,0:T(8,128)(2,1)S(1)}, u32[]{:S(2)}, u32[]{:S(2)}) %collective-permute-start) | collective-permute-done | bytes 1048608 | tf_op jit(solution)/shard_map/while/body/eval_jaxpr/ppermute | solution.py:10
  244.8 1.9 collective-permute-start
  246.7 15.1 %collective-permute-done = bf16[1024,512]{1,0:T(8,128)(2,1)S(1)} collective-permute-done((bf16[1024,512]{1,0:T(8,128)(2,1)S(1)}, bf16[1024,512]{1,0:T(8,128)(2,1)S(1)}, u32[]{:S(2)}, u32[]{:S(2)}) %collective-permute-start) | collective-permute-done | bytes 1048608 | tf_op jit(solution)/shard_map/while/body/eval_jaxpr/ppermute | solution.py:10
  262.0 1.9 collective-permute-start
  263.9 15.1 %collective-permute-done = bf16[1024,512]{1,0:T(8,128)(2,1)S(1)} collective-permute-done((bf16[1024,512]{1,0:T(8,128)(2,1)S(1)}, bf16[1024,512]{1,0:T(8,128)(2,1)S(1)}, u32[]{:S(2)}, u32[]{:S(2)}) %collective-permute-start) | collective-permute-done | bytes 1048608 | tf_op jit(solution)/shard_map/while/body/eval_jaxpr/ppermute | solution.py:10
  279.1 1.9 collective-permute-start
  281.0 15.1 %collective-permute-done = bf16[1024,512]{1,0:T(8,128)(2,1)S(1)} collective-permute-done((bf16[1024,512]{1,0:T(8,128)(2,1)S(1)}, bf16[1024,512]{1,0:T(8,128)(2,1)S(1)}, u32[]{:S(2)}, u32[]{:S(2)}) %collective-permute-start) | collective-permute-done | bytes 1048608 | tf_op jit(solution)/shard_map/while/body/eval_jaxpr/ppermute | solution.py:10
  (19 shorter events, 0.7 us)
Async XLA Ops:
  6.5 122.6 %copy-start = (bf16[1024,512]{1,0:T(8,128)(2,1)S(1)}, bf16[1024,512]{1,0:T(8,128)(2,1)}, u32[]{:S(2)}) copy-start(bf16[1024,512]{1,0:T(8,128)(2,1)} %param.15) | copy-start | bytes 3145732
  6.5 119.1 %all-gather.2.cloned.1.call-start = ((), (), s32[]{:S(2)}) async-start(), calls=%async_computation | async-start | bytes 7864320 | tf_op jit(solution)/shard_map/all_gather | solution.py:35
  129.2 17.0 %collective-permute-start = (bf16[1024,512]{1,0:T(8,128)(2,1)S(1)}, bf16[1024,512]{1,0:T(8,128)(2,1)S(1)}, u32[]{:S(2)}, u32[]{:S(2)}) collective-permute-start(bf16[1024,512]{1,0:T(8,128)(2,1)S(1)} %get-tuple-element.235), channel_id=1, source_target_pairs={{4,0},{8,4},{12,8},{16,12},{20,16},{24,20},{28,24},{5,1},{9,5},{13... | collective-permute-start | bytes 3145736 | tf_op jit(solution)/shard_map/while/body/eval_jaxpr/ppermute | solution.py:10
  146.3 17.0 %collective-permute-start = (bf16[1024,512]{1,0:T(8,128)(2,1)S(1)}, bf16[1024,512]{1,0:T(8,128)(2,1)S(1)}, u32[]{:S(2)}, u32[]{:S(2)}) collective-permute-start(bf16[1024,512]{1,0:T(8,128)(2,1)S(1)} %get-tuple-element.235), channel_id=1, source_target_pairs={{4,0},{8,4},{12,8},{16,12},{20,16},{24,20},{28,24},{5,1},{9,5},{13... | collective-permute-start | bytes 3145736 | tf_op jit(solution)/shard_map/while/body/eval_jaxpr/ppermute | solution.py:10
  163.4 17.0 %collective-permute-start = (bf16[1024,512]{1,0:T(8,128)(2,1)S(1)}, bf16[1024,512]{1,0:T(8,128)(2,1)S(1)}, u32[]{:S(2)}, u32[]{:S(2)}) collective-permute-start(bf16[1024,512]{1,0:T(8,128)(2,1)S(1)} %get-tuple-element.235), channel_id=1, source_target_pairs={{4,0},{8,4},{12,8},{16,12},{20,16},{24,20},{28,24},{5,1},{9,5},{13... | collective-permute-start | bytes 3145736 | tf_op jit(solution)/shard_map/while/body/eval_jaxpr/ppermute | solution.py:10
  180.6 31.8 %collective-permute-start = (bf16[1024,512]{1,0:T(8,128)(2,1)S(1)}, bf16[1024,512]{1,0:T(8,128)(2,1)S(1)}, u32[]{:S(2)}, u32[]{:S(2)}) collective-permute-start(bf16[1024,512]{1,0:T(8,128)(2,1)S(1)} %get-tuple-element.235), channel_id=1, source_target_pairs={{4,0},{8,4},{12,8},{16,12},{20,16},{24,20},{28,24},{5,1},{9,5},{13... | collective-permute-start | bytes 3145736 | tf_op jit(solution)/shard_map/while/body/eval_jaxpr/ppermute | solution.py:10
  227.7 17.0 %collective-permute-start = (bf16[1024,512]{1,0:T(8,128)(2,1)S(1)}, bf16[1024,512]{1,0:T(8,128)(2,1)S(1)}, u32[]{:S(2)}, u32[]{:S(2)}) collective-permute-start(bf16[1024,512]{1,0:T(8,128)(2,1)S(1)} %get-tuple-element.235), channel_id=1, source_target_pairs={{4,0},{8,4},{12,8},{16,12},{20,16},{24,20},{28,24},{5,1},{9,5},{13... | collective-permute-start | bytes 3145736 | tf_op jit(solution)/shard_map/while/body/eval_jaxpr/ppermute | solution.py:10
  244.8 17.0 %collective-permute-start = (bf16[1024,512]{1,0:T(8,128)(2,1)S(1)}, bf16[1024,512]{1,0:T(8,128)(2,1)S(1)}, u32[]{:S(2)}, u32[]{:S(2)}) collective-permute-start(bf16[1024,512]{1,0:T(8,128)(2,1)S(1)} %get-tuple-element.235), channel_id=1, source_target_pairs={{4,0},{8,4},{12,8},{16,12},{20,16},{24,20},{28,24},{5,1},{9,5},{13... | collective-permute-start | bytes 3145736 | tf_op jit(solution)/shard_map/while/body/eval_jaxpr/ppermute | solution.py:10
  262.0 17.0 %collective-permute-start = (bf16[1024,512]{1,0:T(8,128)(2,1)S(1)}, bf16[1024,512]{1,0:T(8,128)(2,1)S(1)}, u32[]{:S(2)}, u32[]{:S(2)}) collective-permute-start(bf16[1024,512]{1,0:T(8,128)(2,1)S(1)} %get-tuple-element.235), channel_id=1, source_target_pairs={{4,0},{8,4},{12,8},{16,12},{20,16},{24,20},{28,24},{5,1},{9,5},{13... | collective-permute-start | bytes 3145736 | tf_op jit(solution)/shard_map/while/body/eval_jaxpr/ppermute | solution.py:10
  279.1 17.0 %collective-permute-start = (bf16[1024,512]{1,0:T(8,128)(2,1)S(1)}, bf16[1024,512]{1,0:T(8,128)(2,1)S(1)}, u32[]{:S(2)}, u32[]{:S(2)}) collective-permute-start(bf16[1024,512]{1,0:T(8,128)(2,1)S(1)} %get-tuple-element.235), channel_id=1, source_target_pairs={{4,0},{8,4},{12,8},{16,12},{20,16},{24,20},{28,24},{5,1},{9,5},{13... | collective-permute-start | bytes 3145736 | tf_op jit(solution)/shard_map/while/body/eval_jaxpr/ppermute | solution.py:10
Sparse Core Ops, SparseCore 0:
  8.9 116.7 all-gather.1
where the time goes:
time: 303 us
  waiting for transfers between devices  254 us (84%)
  starting transfers between devices  15.8 us (5%)
  between operations  13.4 us (4%)
  local copies, waits for them, and re-layouts  8.74 us (3%)
  matrix products  8.52 us (3%)
    ppermute x8, waiting for transfers between devices, from_behind(): return lax.ppermute(block, axis, route)  135 us
    all_gather x1, waiting for transfers between devices, shards(): blocks = lax.all_gather(steps, 'space', axis=1, tiled=True)  118 us
    ppermute x8, starting transfers between devices, from_behind(): return lax.ppermute(block, axis, route)  15.8 us
    dot_general x3, matrix products, live(): value = jnp.dot(blocks[slot], carry_in, preferred_element_type=jnp.float32)  8.52 us
  transfers between devices with their start and end apart: 9, of which 9 were waited for; matrix products, arithmetic and copies ran while one was open for 0% of the time, Pallas kernels for 0%

commit v1 on v0

--- a/solution.py
+++ b/solution.py
@@ -32,7 +32,14 @@
     segments = lax.axis_size("tm")
     me = lax.axis_index("tm")
     section_count = lengths[0]
-    blocks = lax.all_gather(steps, "space", axis=1, tiled=True)
+    ring = [steps]
+    for hop in range(3):
+        ring.append(lax.ppermute(ring[-1], "space", [(dev, (dev + 1) % 4) for dev in range(4)]))
+    blocks = jnp.roll(
+        jnp.concatenate(ring[::-1], axis=1),
+        (lax.axis_index("space") + 1) * ring[0].shape[1],
+        axis=1,
+    )
     results = jnp.zeros((capacity, rows, width), jnp.float32)
 
     def segment(k, state):

time: 303 us -> 293 us (0.967)
  between operations: 13.4 us -> 0.06 us
  waiting for transfers between devices: 254 us -> 243 us
  local copies, waits for them, and re-layouts: 8.74 us -> 18.7 us
  starting transfers between devices: 15.8 us -> 19.7 us
    all_gather x1 -> x0, waiting for transfers between devices: 118 us -> none  [shards(): blocks = lax.all_gather(steps, 'space', axis=1, tiled=True)]
    ppermute x0 -> x3, waiting for transfers between devices: none -> 109 us  [shards(): lax.ppermute(ring[-1], 'space', [(dev, (dev + 1) % 4) for dev in range(4)])]
    unnamed x2 -> x11, local copies, waits for them, and re-layouts: 0.01 us -> 6.48 us
    dynamic_slice x0 -> x1, local copies, waits for them, and re-layouts: none -> 3.38 us  [shards(): jnp.roll(jnp.concatenate(ring[::-1], axis=1), (lax.axis_index('space') +...]
  transfers between devices with their start and end apart: 9 -> 11, of which waited for: 9 -> 11; matrix products, arithmetic and copies ran while one was open for 0% -> 0% of each run, Pallas kernels for 0% -> 0%
where the time goes in v1:
time: 293 us
  waiting for transfers between devices  243 us (83%)
  starting transfers between devices  19.7 us (7%)
  local copies, waits for them, and re-layouts  18.7 us (6%)
  matrix products  8.52 us (3%)
    ppermute x8, waiting for transfers between devices, from_behind(): return lax.ppermute(block, axis, route)  135 us
    ppermute x3, waiting for transfers between devices, shards(): lax.ppermute(ring[-1], 'space', [(dev, (dev + 1) % 4) for dev in range(4)])  109 us
    ppermute x8, starting transfers between devices, from_behind(): return lax.ppermute(block, axis, route)  18.4 us
    dot_general x3, matrix products, live(): value = jnp.dot(blocks[slot], carry_in, preferred_element_type=jnp.float32)  8.52 us
    unnamed x11, local copies, waits for them, and re-layouts  6.48 us
  transfers between devices with their start and end apart: 11, of which 11 were waited for; matrix products, arithmetic and copies ran while one was open for 0% of the time, Pallas kernels for 0%

profile of v1, /device:TPU:3, one launch (start us, length us, event | category | flops | bytes accessed | tf_op | source)
XLA Modules:
  0.0 292.9 jit_solution(15430566792756954722)
XLA Ops:
  1.3 36.3 %collective-permute-done.1 = bf16[3,256,1024]{2,1,0:T(8,128)(2,1)S(1)} collective-permute-done((bf16[3,256,1024]{2,1,0:T(8,128)(2,1)}, bf16[3,256,1024]{2,1,0:T(8,128)(2,1)S(1)}, u32[]{:S(2)}, u32[]{:S(2)}) %collective-permute-start.1) | collective-permute-done | bytes 1572896 | tf_op jit(solution)/shard_map/ppermute | solution.py:37
  37.6 36.5 %collective-permute-done.2 = bf16[3,256,1024]{2,1,0:T(8,128)(2,1)} collective-permute-done((bf16[3,256,1024]{2,1,0:T(8,128)(2,1)S(1)}, bf16[3,256,1024]{2,1,0:T(8,128)(2,1)}, u32[]{:S(2)}, u32[]{:S(2)}) %collective-permute-start.2) | collective-permute-done | bytes 1572896 | tf_op jit(solution)/shard_map/ppermute | solution.py:37
  74.0 35.8 %collective-permute-done.3 = bf16[3,256,1024]{2,1,0:T(8,128)(2,1)} collective-permute-done((bf16[3,256,1024]{2,1,0:T(8,128)(2,1)}, bf16[3,256,1024]{2,1,0:T(8,128)(2,1)}, u32[]{:S(2)}, u32[]{:S(2)}) %collective-permute-start.3) | collective-permute-done | bytes 1572896 | tf_op jit(solution)/shard_map/ppermute | solution.py:37
  111.4 1.5 constant_dynamic-update-slice_fusion.6
  113.2 1.5 constant_dynamic-update-slice_fusion.3
  114.7 1.5 constant_dynamic-update-slice_fusion.2
  116.5 3.4 %constant_dynamic-slice_fusion = bf16[3,1024,1024]{2,1,0:T(8,128)(2,1)} fusion(bf16[3,2048,1024]{2,1,0:T(8,128)(2,1)S(1)} %constant_dynamic-update-slice_fusion, s32[]{:T(128)S(6)} %select_n.14), kind=kLoop, calls=%fused_computation.20 | loop fusion | bytes 12582916 | tf_op jit(solution)/shard_map/jit(_roll_dynamic)/dynamic_slice | solution.py:38
  119.9 3.5 %broadcast_in_dim.12 = f32[3,1024,512]{2,1,0:T(8,128)} broadcast(f32[]{:T(128)} %constant.61.clone.1), dimensions={} | broadcast | bytes 6291460 | tf_op jit(solution)/shard_map/broadcast_in_dim | solution.py:43
  123.4 169.5 %while.15 = (s32[]{:T(128)}, bf16[1024,512]{1,0:T(8,128)(2,1)S(1)}, f32[3,1024,512]{2,1,0:T(8,128)}, s32[]{:T(128)}, s32[]{:T(128)}, /*index=5*/bf16[3,1024,1024]{2,1,0:T(8,128)(2,1)}, s32[]{:T(128)}, s32[]{:T(128)}) while((s32[]{:T(128)}, bf16[1024,512]{1,0:T(8,128)(2,1)S(1)}, f32[3,1024,512]{2,1,0:T(8,128)}, s32[]{:T(128)}, s32[]{:T(128)}, ...), condition=%wide.region_9.10_spmd, body=%wide.region_0.9_spmd.sunk | while | flops 3222798336 | bytes 44040592 | solution.py:57
  123.4 5.0 %collective-permute-start = (bf16[1024,512]{1,0:T(8,128)(2,1)S(1)}, bf16[1024,512]{1,0:T(8,128)(2,1)S(1)}, u32[]{:S(2)}, u32[]{:S(2)}) collective-permute-start(bf16[1024,512]{1,0:T(8,128)(2,1)S(1)} %get-tuple-element.235), channel_id=1, source_target_pairs={{4,0},{8,4},{12,8},{16,12},{20,16},{24,20},{28,24},{5,1},{9,5},{13... | collective-permute-start | bytes 3145736 | tf_op jit(solution)/shard_map/while/body/eval_jaxpr/ppermute | solution.py:10
  128.4 13.6 %collective-permute-done = bf16[1024,512]{1,0:T(8,128)(2,1)S(1)} collective-permute-done((bf16[1024,512]{1,0:T(8,128)(2,1)S(1)}, bf16[1024,512]{1,0:T(8,128)(2,1)S(1)}, u32[]{:S(2)}, u32[]{:S(2)}) %collective-permute-start) | collective-permute-done | bytes 1048608 | tf_op jit(solution)/shard_map/while/body/eval_jaxpr/ppermute | solution.py:10
  142.1 1.9 collective-permute-start
  144.0 15.1 %collective-permute-done = bf16[1024,512]{1,0:T(8,128)(2,1)S(1)} collective-permute-done((bf16[1024,512]{1,0:T(8,128)(2,1)S(1)}, bf16[1024,512]{1,0:T(8,128)(2,1)S(1)}, u32[]{:S(2)}, u32[]{:S(2)}) %collective-permute-start) | collective-permute-done | bytes 1048608 | tf_op jit(solution)/shard_map/while/body/eval_jaxpr/ppermute | solution.py:10
  159.2 1.9 collective-permute-start
  161.1 15.1 %collective-permute-done = bf16[1024,512]{1,0:T(8,128)(2,1)S(1)} collective-permute-done((bf16[1024,512]{1,0:T(8,128)(2,1)S(1)}, bf16[1024,512]{1,0:T(8,128)(2,1)S(1)}, u32[]{:S(2)}, u32[]{:S(2)}) %collective-permute-start) | collective-permute-done | bytes 1048608 | tf_op jit(solution)/shard_map/while/body/eval_jaxpr/ppermute | solution.py:10
  176.3 1.9 collective-permute-start
  178.3 30.8 %collective-permute-done = bf16[1024,512]{1,0:T(8,128)(2,1)S(1)} collective-permute-done((bf16[1024,512]{1,0:T(8,128)(2,1)S(1)}, bf16[1024,512]{1,0:T(8,128)(2,1)S(1)}, u32[]{:S(2)}, u32[]{:S(2)}) %collective-permute-start) | collective-permute-done | bytes 1048608 | tf_op jit(solution)/shard_map/while/body/eval_jaxpr/ppermute | solution.py:10
  209.1 15.3 %conditional.5 = ((bf16[1024,512]{1,0:T(8,128)(2,1)S(1)}, f32[3,1024,512]{2,1,0:T(8,128)})) conditional(s32[]{:T(128)} %convert_element_type.29, (bf16[1024,512]{1,0:T(8,128)(2,1)S(1)}, f32[3,1024,512]{2,1,0:T(8,128)}) %tuple.58, (s32[]{:T(128)}, bf16[1024,512]{1,0:T(8,128)(2,1)S(1)}, f32[3,1024,512]{2,1,0:T(8,128)}, ...), branch_computations={%region_1.1_spmd, %region_2.8_spmd} | conditional | flops 3222798336 | bytes 37748936 | solution.py:48
  209.8 4.4 %conditional = ((bf16[1024,512]{1,0:T(8,128)(2,1)S(1)}, f32[3,1024,512]{2,1,0:T(8,128)})) conditional(s32[]{:T(128)} %convert_element_type.23, (bf16[1024,512]{1,0:T(8,128)(2,1)S(1)}, f32[3,1024,512]{2,1,0:T(8,128)}) %tuple.36, (bf16[3,1024,1024]{2,1,0:T(8,128)(2,1)}, bf16[1024,512]{1,0:T(8,128)(2,1)S(1)}, f32[3,1024,512]{2,1,0:T(8,128)}) %tuple.37), branch_computations={%region_3.2_spmd, %region_4.3_spmd} | conditional | flops 1074266112 | bytes 12582936 | solution.py:23
  209.9 2.8 fusion.9
  214.9 4.4 %conditional.1 = ((bf16[1024,512]{1,0:T(8,128)(2,1)S(1)}, f32[3,1024,512]{2,1,0:T(8,128)})) conditional(s32[]{:T(128)} %convert_element_type.22, (bf16[1024,512]{1,0:T(8,128)(2,1)S(1)}, f32[3,1024,512]{2,1,0:T(8,128)}) %get-tuple-element.277, (bf16[3,1024,1024]{2,1,0:T(8,128)(2,1)}, bf16[1024,512]{1,0:T(8,128)(2,1)S(1)}, ...), branch_computations={%region_5.4_spmd, %region_6.5_spmd} | conditional | flops 1074266112 | bytes 12582936 | solution.py:23
  215.0 2.8 fusion.10
  220.0 4.4 %conditional.2 = ((bf16[1024,512]{1,0:T(8,128)(2,1)S(1)}, f32[3,1024,512]{2,1,0:T(8,128)})) conditional(s32[]{:T(128)} %convert_element_type.21, (bf16[1024,512]{1,0:T(8,128)(2,1)S(1)}, f32[3,1024,512]{2,1,0:T(8,128)}) %get-tuple-element.278, (bf16[3,1024,1024]{2,1,0:T(8,128)(2,1)}, bf16[1024,512]{1,0:T(8,128)(2,1)S(1)}, ...), branch_computations={%region_7.6_spmd, %region_8.7_spmd} | conditional | flops 1074266112 | bytes 12582936 | solution.py:23
  220.0 2.8 fusion.11
  224.4 1.9 collective-permute-start
  226.3 15.1 %collective-permute-done = bf16[1024,512]{1,0:T(8,128)(2,1)S(1)} collective-permute-done((bf16[1024,512]{1,0:T(8,128)(2,1)S(1)}, bf16[1024,512]{1,0:T(8,128)(2,1)S(1)}, u32[]{:S(2)}, u32[]{:S(2)}) %collective-permute-start) | collective-permute-done | bytes 1048608 | tf_op jit(solution)/shard_map/while/body/eval_jaxpr/ppermute | solution.py:10
  241.5 1.9 collective-permute-start
  243.4 15.1 %collective-permute-done = bf16[1024,512]{1,0:T(8,128)(2,1)S(1)} collective-permute-done((bf16[1024,512]{1,0:T(8,128)(2,1)S(1)}, bf16[1024,512]{1,0:T(8,128)(2,1)S(1)}, u32[]{:S(2)}, u32[]{:S(2)}) %collective-permute-start) | collective-permute-done | bytes 1048608 | tf_op jit(solution)/shard_map/while/body/eval_jaxpr/ppermute | solution.py:10
  258.6 1.9 collective-permute-start
  260.6 15.1 %collective-permute-done = bf16[1024,512]{1,0:T(8,128)(2,1)S(1)} collective-permute-done((bf16[1024,512]{1,0:T(8,128)(2,1)S(1)}, bf16[1024,512]{1,0:T(8,128)(2,1)S(1)}, u32[]{:S(2)}, u32[]{:S(2)}) %collective-permute-start) | collective-permute-done | bytes 1048608 | tf_op jit(solution)/shard_map/while/body/eval_jaxpr/ppermute | solution.py:10
  275.8 1.9 collective-permute-start
  277.7 15.1 %collective-permute-done = bf16[1024,512]{1,0:T(8,128)(2,1)S(1)} collective-permute-done((bf16[1024,512]{1,0:T(8,128)(2,1)S(1)}, bf16[1024,512]{1,0:T(8,128)(2,1)S(1)}, u32[]{:S(2)}, u32[]{:S(2)}) %collective-permute-start) | collective-permute-done | bytes 1048608 | tf_op jit(solution)/shard_map/while/body/eval_jaxpr/ppermute | solution.py:10
  (33 shorter events, 8.6 us)
Async XLA Ops:
  0.0 113.0 %copy-start.1 = (bf16[3,256,1024]{2,1,0:T(8,128)(2,1)S(1)}, bf16[3,256,1024]{2,1,0:T(8,128)(2,1)}, u32[]{:S(2)}) copy-start(bf16[3,256,1024]{2,1,0:T(8,128)(2,1)} %param.13) | copy-start | bytes 4718596
  0.0 37.6 %collective-permute-start.1 = (bf16[3,256,1024]{2,1,0:T(8,128)(2,1)}, bf16[3,256,1024]{2,1,0:T(8,128)(2,1)S(1)}, u32[]{:S(2)}, u32[]{:S(2)}) collective-permute-start(bf16[3,256,1024]{2,1,0:T(8,128)(2,1)} %param.13), channel_id=1, source_target_pairs={{0,1},{1,2},{2,3},{3,0},{4,5},{5,6},{6,7},{7,4},{8,9},{9,10},{10,1... | collective-permute-start | bytes 4718600 | tf_op jit(solution)/shard_map/ppermute | solution.py:37
  37.6 36.5 %collective-permute-start.2 = (bf16[3,256,1024]{2,1,0:T(8,128)(2,1)S(1)}, bf16[3,256,1024]{2,1,0:T(8,128)(2,1)}, u32[]{:S(2)}, u32[]{:S(2)}) collective-permute-start(bf16[3,256,1024]{2,1,0:T(8,128)(2,1)S(1)} %collective-permute-done.1), channel_id=1, source_target_pairs={{0,1},{1,2},{2,3},{3,0},{4,5},{5,6},{6,7},{7,4},{8,9},{9,10},{10,1... | collective-permute-start | bytes 4718600 | tf_op jit(solution)/shard_map/ppermute | solution.py:37
  74.0 35.8 %collective-permute-start.3 = (bf16[3,256,1024]{2,1,0:T(8,128)(2,1)}, bf16[3,256,1024]{2,1,0:T(8,128)(2,1)}, u32[]{:S(2)}, u32[]{:S(2)}) collective-permute-start(bf16[3,256,1024]{2,1,0:T(8,128)(2,1)} %collective-permute-done.2), channel_id=1, source_target_pairs={{0,1},{1,2},{2,3},{3,0},{4,5},{5,6},{6,7},{7,4},{8,9},{9,10},{10,1... | collective-permute-start | bytes 4718600 | tf_op jit(solution)/shard_map/ppermute | solution.py:37
  119.9 3.5 %copy-start = (bf16[1024,512]{1,0:T(8,128)(2,1)S(1)}, bf16[1024,512]{1,0:T(8,128)(2,1)}, u32[]{:S(2)}) copy-start(bf16[1024,512]{1,0:T(8,128)(2,1)} %param.15) | copy-start | bytes 3145732
  123.4 18.6 %collective-permute-start = (bf16[1024,512]{1,0:T(8,128)(2,1)S(1)}, bf16[1024,512]{1,0:T(8,128)(2,1)S(1)}, u32[]{:S(2)}, u32[]{:S(2)}) collective-permute-start(bf16[1024,512]{1,0:T(8,128)(2,1)S(1)} %get-tuple-element.235), channel_id=1, source_target_pairs={{4,0},{8,4},{12,8},{16,12},{20,16},{24,20},{28,24},{5,1},{9,5},{13... | collective-permute-start | bytes 3145736 | tf_op jit(solution)/shard_map/while/body/eval_jaxpr/ppermute | solution.py:10
  142.1 17.0 %collective-permute-start = (bf16[1024,512]{1,0:T(8,128)(2,1)S(1)}, bf16[1024,512]{1,0:T(8,128)(2,1)S(1)}, u32[]{:S(2)}, u32[]{:S(2)}) collective-permute-start(bf16[1024,512]{1,0:T(8,128)(2,1)S(1)} %get-tuple-element.235), channel_id=1, source_target_pairs={{4,0},{8,4},{12,8},{16,12},{20,16},{24,20},{28,24},{5,1},{9,5},{13... | collective-permute-start | bytes 3145736 | tf_op jit(solution)/shard_map/while/body/eval_jaxpr/ppermute | solution.py:10
  159.2 17.0 %collective-permute-start = (bf16[1024,512]{1,0:T(8,128)(2,1)S(1)}, bf16[1024,512]{1,0:T(8,128)(2,1)S(1)}, u32[]{:S(2)}, u32[]{:S(2)}) collective-permute-start(bf16[1024,512]{1,0:T(8,128)(2,1)S(1)} %get-tuple-element.235), channel_id=1, source_target_pairs={{4,0},{8,4},{12,8},{16,12},{20,16},{24,20},{28,24},{5,1},{9,5},{13... | collective-permute-start | bytes 3145736 | tf_op jit(solution)/shard_map/while/body/eval_jaxpr/ppermute | solution.py:10
  176.3 32.7 %collective-permute-start = (bf16[1024,512]{1,0:T(8,128)(2,1)S(1)}, bf16[1024,512]{1,0:T(8,128)(2,1)S(1)}, u32[]{:S(2)}, u32[]{:S(2)}) collective-permute-start(bf16[1024,512]{1,0:T(8,128)(2,1)S(1)} %get-tuple-element.235), channel_id=1, source_target_pairs={{4,0},{8,4},{12,8},{16,12},{20,16},{24,20},{28,24},{5,1},{9,5},{13... | collective-permute-start | bytes 3145736 | tf_op jit(solution)/shard_map/while/body/eval_jaxpr/ppermute | solution.py:10
  224.4 17.0 %collective-permute-start = (bf16[1024,512]{1,0:T(8,128)(2,1)S(1)}, bf16[1024,512]{1,0:T(8,128)(2,1)S(1)}, u32[]{:S(2)}, u32[]{:S(2)}) collective-permute-start(bf16[1024,512]{1,0:T(8,128)(2,1)S(1)} %get-tuple-element.235), channel_id=1, source_target_pairs={{4,0},{8,4},{12,8},{16,12},{20,16},{24,20},{28,24},{5,1},{9,5},{13... | collective-permute-start | bytes 3145736 | tf_op jit(solution)/shard_map/while/body/eval_jaxpr/ppermute | solution.py:10
  241.5 17.0 %collective-permute-start = (bf16[1024,512]{1,0:T(8,128)(2,1)S(1)}, bf16[1024,512]{1,0:T(8,128)(2,1)S(1)}, u32[]{:S(2)}, u32[]{:S(2)}) collective-permute-start(bf16[1024,512]{1,0:T(8,128)(2,1)S(1)} %get-tuple-element.235), channel_id=1, source_target_pairs={{4,0},{8,4},{12,8},{16,12},{20,16},{24,20},{28,24},{5,1},{9,5},{13... | collective-permute-start | bytes 3145736 | tf_op jit(solution)/shard_map/while/body/eval_jaxpr/ppermute | solution.py:10
  258.6 17.0 %collective-permute-start = (bf16[1024,512]{1,0:T(8,128)(2,1)S(1)}, bf16[1024,512]{1,0:T(8,128)(2,1)S(1)}, u32[]{:S(2)}, u32[]{:S(2)}) collective-permute-start(bf16[1024,512]{1,0:T(8,128)(2,1)S(1)} %get-tuple-element.235), channel_id=1, source_target_pairs={{4,0},{8,4},{12,8},{16,12},{20,16},{24,20},{28,24},{5,1},{9,5},{13... | collective-permute-start | bytes 3145736 | tf_op jit(solution)/shard_map/while/body/eval_jaxpr/ppermute | solution.py:10
  275.8 17.0 %collective-permute-start = (bf16[1024,512]{1,0:T(8,128)(2,1)S(1)}, bf16[1024,512]{1,0:T(8,128)(2,1)S(1)}, u32[]{:S(2)}, u32[]{:S(2)}) collective-permute-start(bf16[1024,512]{1,0:T(8,128)(2,1)S(1)} %get-tuple-element.235), channel_id=1, source_target_pairs={{4,0},{8,4},{12,8},{16,12},{20,16},{24,20},{28,24},{5,1},{9,5},{13... | collective-permute-start | bytes 3145736 | tf_op jit(solution)/shard_map/while/body/eval_jaxpr/ppermute | solution.py:10
